TPU v7x, 512 devices: a whole 4x8x8 slice. The times are simulated.
512 devices in a mesh: ep: 64 (over z, y), tp: 8 (over x, core).
Axes of the slice: x: 4, y: 8, z: 8, core: 2. Of those that a mesh axis runs over, the one named last changes fastest.
Arguments:
- patches: bfloat16 [32768, 1024], P('ep', 'tp'), may hold values from -6 to 6
- patch_grad: bfloat16 [32768, 1024], P('ep', 'tp'), may hold values from -1.796875 to 1.796875
- expert_up: bfloat16 [64, 1024, 4096], P('ep', None, 'tp'), may hold values from -0.1875 to 0.1875
- expert_down: bfloat16 [64, 4096, 1024], P('ep', 'tp'), may hold values from -0.09375 to 0.09375
- expert_counts: int32 [64, 64], P('ep'), may hold values from 1 to 16, as said below
Outputs:
- input_grad: bfloat16 [32768, 1024], P('ep', 'tp')
- up_grad: bfloat16 [64, 1024, 4096], P('ep', None, 'tp')
- down_grad: bfloat16 [64, 4096, 1024], P('ep', 'tp')
Inputs may be any that keep to these rules, and one draw needn't show every extreme that they name: `expert_counts`: row s gives, for each of the 64 experts in order, how many of the 512 rows of ep index s are routed to it; those rows stand together in expert order. Every row sums to 512, and one expert has exactly 16 rows from every index of ep.
All inputs are finite; a program needn't handle non-finite values.
Results may differ from a plain program's by a relative error of at most 0.0049.
Values may be sent and summed in bfloat16 or wider, within the bound.
No kernel may reach another device: no remote copies, remote signals or barrier semaphores. Data moves between devices by JAX's collectives and lax.ppermute only.
A program may use at most 64 MiB of HBM per device.

v0:
```python
import jax
import jax.numpy as jnp
from jax import lax
from jax.sharding import PartitionSpec as P


def activation(values):
    return jax.nn.gelu(values, approximate=True)


def slot_plan(counts_row, row_count, capacity):
    experts = counts_row.shape[0]
    row_ends = jnp.cumsum(counts_row)
    row_starts = row_ends - counts_row
    positions = lax.broadcasted_iota(jnp.int32, (experts, capacity), 1)
    slot_live = positions < counts_row[:, None]
    slot_source = jnp.where(slot_live, row_starts[:, None] + positions, 0)
    row_ids = lax.broadcasted_iota(jnp.int32, (row_count, experts), 0)
    row_expert = jnp.sum((row_ids >= row_ends[None, :]).astype(jnp.int32), axis=1)
    expert_ids = lax.broadcasted_iota(jnp.int32, (row_count, experts), 1)
    own_start = jnp.sum(
        jnp.where(row_expert[:, None] == expert_ids, row_starts[None, :], 0), axis=1
    )
    row_numbers = lax.broadcasted_iota(jnp.int32, (row_count,), 0)
    row_slot = row_expert * capacity + row_numbers - own_start
    return (slot_live, slot_source, row_slot)


def fill_slots(source_table, slot_live, slot_source):
    picked = jnp.take(source_table, slot_source.reshape(-1), axis=0)
    picked = picked.reshape(slot_source.shape + (source_table.shape[1],))
    return jnp.where(slot_live[:, :, None], picked, jnp.zeros((), source_table.dtype))


def per_device(patches, patch_grad, expert_up, expert_down, expert_counts):
    row_count = patches.shape[0]
    experts = expert_counts.shape[1]
    capacity = 2 * row_count // experts
    slot_live, slot_source, row_slot = slot_plan(expert_counts[0], row_count, capacity)
    weight_up = expert_up[0]
    weight_down = expert_down[0]
    gathered_rows, gathered_grads = (
        lax.all_gather(patches, "tp", axis=1, tiled=True),
        lax.all_gather(patch_grad, "tp", axis=1, tiled=True),
    )
    send_rows = fill_slots(gathered_rows, slot_live, slot_source)
    send_grads = fill_slots(gathered_grads, slot_live, slot_source)
    got_rows, got_grads = (
        lax.all_to_all(send_rows, "ep", split_axis=0, concat_axis=0, tiled=True),
        lax.all_to_all(send_grads, "ep", split_axis=0, concat_axis=0, tiled=True),
    )
    sources = got_rows.shape[0]
    feature_width = got_rows.shape[2]
    slot_rows = got_rows.reshape(sources * capacity, feature_width)
    slot_grads = got_grads.reshape(sources * capacity, feature_width)
    pre_act = jnp.dot(slot_rows, weight_up, preferred_element_type=jnp.float32)
    act_value, act_back = jax.vjp(activation, pre_act)
    hidden = act_value.astype(jnp.bfloat16)
    hidden_grad = lax.dot_general(
        slot_grads, weight_down, (((1,), (1,)), ((), ())), preferred_element_type=jnp.float32
    )
    pre_grad = act_back(hidden_grad)[0].astype(jnp.bfloat16)
    down_part = lax.dot_general(
        hidden, slot_grads, (((0,), (0,)), ((), ())), preferred_element_type=jnp.float32
    )
    up_part = lax.dot_general(
        slot_rows, pre_grad, (((0,), (0,)), ((), ())), preferred_element_type=jnp.float32
    )
    row_term = lax.dot_general(
        pre_grad, weight_up, (((1,), (1,)), ((), ())), preferred_element_type=jnp.float32
    )
    summed = lax.psum_scatter(row_term, "tp", scatter_dimension=1, tiled=True)
    back_rows = summed.astype(jnp.bfloat16).reshape(sources, capacity, summed.shape[1])
    returned = lax.all_to_all(back_rows, "ep", split_axis=0, concat_axis=0, tiled=True)
    input_grad = jnp.take(returned.reshape(experts * capacity, returned.shape[2]), row_slot, axis=0)
    return (input_grad, up_part.astype(jnp.bfloat16)[None], down_part.astype(jnp.bfloat16)[None])


def solution(mesh):
    return jax.shard_map(
        per_device,
        mesh=mesh,
        in_specs=(
            P("ep", "tp"),
            P("ep", "tp"),
            P("ep", None, "tp"),
            P("ep", "tp", None),
            P("ep", None),
        ),
        out_specs=(P("ep", "tp"), P("ep", None, "tp"), P("ep", "tp", None)),
        check_vma=False,
    )
```

profile of v0, /device:TPU:8, one launch (start us, length us, event | category | flops | bytes accessed | tf_op | source)
XLA Modules:
  0.0 298.1 jit_solution(2394442050553680179)
XLA Ops:
  7.2 0.7 all-gather.3.cloned.1.call-update
  8.0 0.7 all-gather.5.cloned.1.call-update
  8.7 0.7 copy.10
  9.4 0.1 reduce-window.4
  9.5 0.1 reduce
  9.6 0.7 bitcast_subtract_fusion.1
  10.3 0.7 add_select_fusion
  11.1 0.7 iota_compare_fusion.2
  11.9 31.4 %all-gather.3.cloned.1.call-done = bf16[512,1024]{1,0:T(8,128)(2,1)} async-done(((bf16[512,128]{1,0:T(8,128)(2,1)}), bf16[512,1024]{1,0:T(8,128)(2,1)}) %all-gather.3.cloned.1.call-update) | async-done | bytes 1048592 | tf_op jit(solution)/shard_map/all_gather | solution.py:44
  43.3 6.3 %gather_fusion.1 = bf16[1024,1024]{1,0:T(8,128)(2,1)S(1)} fusion(bf16[512,1024]{1,0:T(8,128)(2,1)} %all-gather.3.cloned.1.call-done, s32[1024]{0:T(1024)S(1)} %fusion.21), kind=kCustom, calls=%fused_computation.clone | custom fusion | bytes 4198400 | tf_op jit(solution)/shard_map/jit(_take)/gather | solution.py:30
  49.6 25.4 %all-gather.5.cloned.1.call-done = bf16[512,1024]{1,0:T(8,128)(2,1)} async-done(((bf16[512,128]{1,0:T(8,128)(2,1)}), bf16[512,1024]{1,0:T(8,128)(2,1)}) %all-gather.5.cloned.1.call-update) | async-done | bytes 1048592 | tf_op jit(solution)/shard_map/all_gather | solution.py:43
  75.0 7.4 %gather_fusion.2 = bf16[1024,1024]{1,0:T(8,128)(2,1)} fusion(bf16[512,1024]{1,0:T(8,128)(2,1)} %all-gather.5.cloned.1.call-done, s32[1024]{0:T(1024)S(1)} %fusion.21), kind=kCustom, calls=%fused_computation.1.clone | custom fusion | bytes 4198400 | tf_op jit(solution)/shard_map/jit(_take)/gather | solution.py:30
  82.4 2.0 broadcast_select_fusion.1
  84.5 1.7 broadcast_select_fusion.3
  86.2 66.0 %all_to_all.15 = bf16[64,16,1024]{2,1,0:T(8,128)(2,1)S(1)} all-to-all(bf16[64,16,1024]{2,1,0:T(8,128)(2,1)S(1)} %get-tuple-element.5), channel_id=1, replica_groups=mesh['ep'=64,'tp'=8] {'ep'}, dimensions={0} | all-to-all | bytes 4194304 | tf_op jit(solution)/shard_map/all_to_all | solution.py:49
  152.2 8.6 %all-to-all-start = ((bf16[64,16,1024]{2,1,0:T(8,128)(2,1)}), bf16[64,16,1024]{2,1,0:T(8,128)(2,1)}, u32[]{:S(2)}, u32[]{:S(2)}) async-start(bf16[64,16,1024]{2,1,0:T(8,128)(2,1)} %get-tuple-element.4), calls=%async_computation | async-start | bytes 4194304 | tf_op jit(solution)/shard_map/all_to_all | solution.py:50
  160.8 2.6 fusion.11
  163.4 49.6 %all-to-all-done = bf16[64,16,1024]{2,1,0:T(8,128)(2,1)} async-done(((bf16[64,16,1024]{2,1,0:T(8,128)(2,1)}), bf16[64,16,1024]{2,1,0:T(8,128)(2,1)}, u32[]{:S(2)}, u32[]{:S(2)}) %all-to-all-start) | async-done | bytes 2097184 | tf_op jit(solution)/shard_map/all_to_all | solution.py:50
  213.0 4.9 %fusion.6 = bf16[1024,512]{1,0:T(8,128)(2,1)S(1)} fusion(f32[1024,512]{1,0:T(8,128)} %fusion.11, bf16[1024,1024]{1,0:T(8,128)(2,1)} %bitcast.4, bf16[1,512,1024]{2,1,0:T(8,128)(2,1)} %param.10), kind=kOutput, calls=%fused_computation.11 | convolution fusion | flops 1084227584 | bytes 6291456 | tf_op jit(solution)/shard_map/dot_general | solution.py:59
  217.9 1.0 copy-done.2
  218.9 3.2 %fusion.9 = f32[1024,1024]{1,0:T(8,128)} fusion(bf16[1024,512]{1,0:T(8,128)(2,1)S(1)} %fusion.6, bf16[1,1024,512]{2,1,0:T(8,128)(2,1)S(1)} %copy-done), kind=kOutput, calls=%fused_computation.21 | convolution fusion | flops 1073741824 | bytes 6291456 | tf_op jit(solution)/shard_map/dot_general | solution.py:69
  222.1 0.1 convert_reduce_fusion
  222.2 0.5 copy-done.1
  222.8 0.1 select_reduce_fusion
  222.9 38.3 %reduce-scatter.2.cloned.1.call-done = f32[1024,128]{1,0:T(8,128)} async-done(((f32[1024,1024]{1,0:T(8,128)}), f32[1024,128]{1,0:T(8,128)}) %reduce-scatter.2.cloned.1.call-update) | async-done | bytes 524304 | tf_op jit(solution)/shard_map/reduce_scatter | solution.py:72
  261.2 1.8 convert_element_type.20
  263.0 13.4 %all-to-all-start.2 = ((bf16[64,16,128]{2,1,0:T(8,128)(2,1)}), bf16[64,16,128]{2,1,0:T(8,128)(2,1)S(1)}, u32[]{:S(2)}, u32[]{:S(2)}) async-start(bf16[64,16,128]{2,1,0:T(8,128)(2,1)} %bitcast.43), calls=%async_computation.3 | async-start | bytes 524288 | tf_op jit(solution)/shard_map/all_to_all | solution.py:74
  276.4 3.6 %fusion.7 = bf16[1,1024,512]{2,1,0:T(8,128)(2,1)} fusion(bf16[1024,1024]{1,0:T(8,128)(2,1)S(1)} %bitcast.42, bf16[1024,512]{1,0:T(8,128)(2,1)} %copy-done.2), kind=kOutput, calls=%fused_computation.19 | convolution fusion | flops 1074266112 | bytes 4194304 | tf_op jit(solution)/shard_map/dot_general | solution.py:66
  280.0 4.0 %fusion.8 = bf16[1,512,1024]{2,1,0:T(8,128)(2,1)} fusion(bf16[1024,1024]{1,0:T(8,128)(2,1)} %bitcast.4, f32[1024,512]{1,0:T(8,128)S(1)} %copy-done.3), kind=kOutput, calls=%fused_computation.20 | convolution fusion | flops 1078984704 | bytes 5242880 | tf_op jit(solution)/shard_map/dot_general | solution.py:63
  284.0 5.4 %all-to-all-done.2 = bf16[64,16,128]{2,1,0:T(8,128)(2,1)S(1)} async-done(((bf16[64,16,128]{2,1,0:T(8,128)(2,1)}), bf16[64,16,128]{2,1,0:T(8,128)(2,1)S(1)}, u32[]{:S(2)}, u32[]{:S(2)}) %all-to-all-start.2) | async-done | bytes 262176 | tf_op jit(solution)/shard_map/all_to_all | solution.py:74
  289.4 1.3 gather_fusion
  290.8 0.8 broadcast_select_fusion.4
  (18 shorter events, 0.3 us)
Async XLA Ops:
  7.2 153.7 %copy-start = (bf16[1,1024,512]{2,1,0:T(8,128)(2,1)S(1)}, bf16[1,1024,512]{2,1,0:T(8,128)(2,1)}, u32[]{:S(2)}) copy-start(bf16[1,1024,512]{2,1,0:T(8,128)(2,1)} %param.9) | copy-start | bytes 3145732
  7.2 36.1 %all-gather.3.cloned.1.call-start = ((), (), s32[]{:S(2)}) async-start(), calls=%async_computation.4 | async-start | bytes 1179648 | tf_op jit(solution)/shard_map/all_gather | solution.py:44
  7.9 67.1 %all-gather.5.cloned.1.call-start = ((), (), s32[]{:S(2)}) async-start(), calls=%async_computation.5 | async-start | bytes 1179648 | tf_op jit(solution)/shard_map/all_gather | solution.py:43
  152.2 60.8 %all-to-all-start = ((bf16[64,16,1024]{2,1,0:T(8,128)(2,1)}), bf16[64,16,1024]{2,1,0:T(8,128)(2,1)}, u32[]{:S(2)}, u32[]{:S(2)}) async-start(bf16[64,16,1024]{2,1,0:T(8,128)(2,1)} %get-tuple-element.4), calls=%async_computation | async-start | bytes 4194304 | tf_op jit(solution)/shard_map/all_to_all | solution.py:50
  160.8 100.5 %reduce-scatter.2.cloned.1.call-start = ((), (), s32[]{:S(2)}) async-start(), calls=%async_computation.6 | async-start | bytes 4718592 | tf_op jit(solution)/shard_map/reduce_scatter | solution.py:72
  217.9 1.0 copy-start.2
  222.1 0.7 copy-start.1
  263.0 26.4 %all-to-all-start.2 = ((bf16[64,16,128]{2,1,0:T(8,128)(2,1)}), bf16[64,16,128]{2,1,0:T(8,128)(2,1)S(1)}, u32[]{:S(2)}, u32[]{:S(2)}) async-start(bf16[64,16,128]{2,1,0:T(8,128)(2,1)} %bitcast.43), calls=%async_computation.3 | async-start | bytes 524288 | tf_op jit(solution)/shard_map/all_to_all | solution.py:74
  276.4 3.6 %copy-start.3 = (f32[1024,512]{1,0:T(8,128)S(1)}, f32[1024,512]{1,0:T(8,128)}, u32[]{:S(2)}) copy-start(f32[1024,512]{1,0:T(8,128)} %fusion.11) | copy-start | bytes 6291460
Sparse Core Ops, SparseCore 0:
  10.1 33.1 all-gather.2
  45.4 29.5 all-gather.4
  222.3 38.9 reduce-scatter.1
where the time goes:
time: 299 us; the launch traced here: 298 us
  waiting for transfers between devices  152 us (51%)
  blocking collectives  66 us (22%)
  starting transfers between devices  22.1 us (7%)
  matrix products  18.3 us (6%)
  local copies, waits for them, and re-layouts  17.4 us (6%)
  between operations  13.9 us (5%)
  other arithmetic  8.85 us (3%)
    all_to_all x1, blocking collectives, per_device(): lax.all_to_all(send_rows, 'ep', split_axis=0, concat_axis=0, tiled=True)  66 us
    all_to_all x1, waiting for transfers between devices, per_device(): lax.all_to_all(send_grads, 'ep', split_axis=0, concat_axis=0, tiled=True)  49.6 us
    reduce_scatter x1, waiting for transfers between devices, per_device(): summed = lax.psum_scatter(row_term, 'tp', scatter_dimension=1, tiled=True)  38.3 us
    all_gather x1, waiting for transfers between devices, per_device(): lax.all_gather(patch_grad, 'tp', axis=1, tiled=True)  31.4 us
    all_gather x1, waiting for transfers between devices, per_device(): lax.all_gather(patches, 'tp', axis=1, tiled=True)  25.4 us
    gather x2, local copies, waits for them, and re-layouts, fill_slots(): picked = jnp.take(source_table, slot_source.reshape(-1), axis=0)  13.7 us
    all_to_all x1, starting transfers between devices, per_device(): lax.all_to_all(back_rows, 'ep', split_axis=0, concat_axis=0, tiled=True)  13.4 us
    all_to_all x1, starting transfers between devices, per_device(): lax.all_to_all(send_grads, 'ep', split_axis=0, concat_axis=0, tiled=True)  8.57 us
  transfers between devices with their start and end apart: 5, of which 5 were waited for; matrix products, arithmetic and copies ran while one was open for 7% of the time, Pallas kernels for 0%

commit v1 on v0

--- a/solution.py
+++ b/solution.py
@@ -2,6 +2,19 @@
 import jax.numpy as jnp
 from jax import lax
 from jax.sharding import PartitionSpec as P
+
+
+def plate_guide(original):
+    opened = jnp.concatenate(
+        jax.lax.all_to_all(
+            jnp.stack([original for _ in range(jax.lax.axis_size("tp"))], axis=0),
+            axis_name="tp",
+            split_axis=0,
+            concat_axis=0,
+        ),
+        1,
+    )
+    return opened
 
 
 def activation(values):
@@ -40,7 +53,7 @@
     weight_up = expert_up[0]
     weight_down = expert_down[0]
     gathered_rows, gathered_grads = (
-        lax.all_gather(patches, "tp", axis=1, tiled=True),
+        plate_guide(patches),
         lax.all_gather(patch_grad, "tp", axis=1, tiled=True),
     )
     send_rows = fill_slots(gathered_rows, slot_live, slot_source)

time: 299 us -> 267 us (0.89)
  waiting for transfers between devices: 152 us -> 117 us
  starting transfers between devices: 22.1 us -> 26.3 us
    all_gather x1 -> x0, waiting for transfers between devices: 25.4 us -> none  [per_device(): lax.all_gather(patches, 'tp', axis=1, tiled=True)]
    all_gather x1, waiting for transfers between devices: 31.4 us -> 7.62 us  [per_device(): lax.all_gather(patch_grad, 'tp', axis=1, tiled=True)]
    all_to_all x0 -> x1, waiting for transfers between devices: none -> 15.3 us  [plate_guide(): jax.lax.all_to_all(jnp.stack([original for _ in range(jax.lax.axis_size('...]
    all_to_all x0 -> x1, starting transfers between devices: none -> 4.3 us  [plate_guide(): jax.lax.all_to_all(jnp.stack([original for _ in range(jax.lax.axis_size('...]
where the time goes in v1:
time: 267 us
  waiting for transfers between devices  117 us (44%)
  blocking collectives  66.2 us (25%)
  starting transfers between devices  26.3 us (10%)
  matrix products  18.3 us (7%)
  local copies, waits for them, and re-layouts  17.4 us (7%)
  between operations  14.2 us (5%)
  other arithmetic  6.88 us (3%)
    all_to_all x1, blocking collectives, per_device(): lax.all_to_all(send_rows, 'ep', split_axis=0, concat_axis=0, tiled=True)  66.2 us
    all_to_all x1, waiting for transfers between devices, per_device(): lax.all_to_all(send_grads, 'ep', split_axis=0, concat_axis=0, tiled=True)  49.5 us
    reduce_scatter x1, waiting for transfers between devices, per_device(): summed = lax.psum_scatter(row_term, 'tp', scatter_dimension=1, tiled=True)  38.8 us
    all_to_all x1, waiting for transfers between devices, plate_guide(): jax.lax.all_to_all(jnp.stack([original for _ in range(jax.lax.axis_size('...  15.3 us
    all_to_all x1, starting transfers between devices, per_device(): lax.all_to_all(back_rows, 'ep', split_axis=0, concat_axis=0, tiled=True)  13.4 us
    gather x2, local copies, waits for them, and re-layouts, fill_slots(): picked = jnp.take(source_table, slot_source.reshape(-1), axis=0)  12.7 us
    all_to_all x1, starting transfers between devices, per_device(): lax.all_to_all(send_grads, 'ep', split_axis=0, concat_axis=0, tiled=True)  8.57 us
    all_gather x1, waiting for transfers between devices, per_device(): lax.all_gather(patch_grad, 'tp', axis=1, tiled=True)  7.62 us
  transfers between devices with their start and end apart: 5, of which 5 were waited for; matrix products, arithmetic and copies ran while one was open for 7% of the time, Pallas kernels for 0%

profile of v1, /device:TPU:8, one launch (start us, length us, event | category | flops | bytes accessed | tf_op | source)
XLA Modules:
  0.0 266.8 jit_solution(1678048613685465293)
XLA Ops:
  7.2 0.7 all-gather.2.cloned.1.call-update
  7.9 2.0 stack.2
  9.9 4.3 %all-to-all-start.1 = ((bf16[8,512,128]{2,1,0:T(8,128)(2,1)}), bf16[8,512,128]{2,1,0:T(8,128)(2,1)S(1)}, u32[]{:S(2)}, u32[]{:S(2)}) async-start(bf16[8,512,128]{2,1,0:T(8,128)(2,1)} %stack.2), calls=%async_computation.1 | async-start | bytes 2097152 | tf_op jit(solution)/shard_map/all_to_all | solution.py:9
  14.2 0.1 copy.12
  14.3 0.1 reduce-window.4
  14.4 0.1 reduce
  14.6 0.1 add_select_fusion
  14.7 0.1 select_n.49
  14.8 15.3 %all-to-all-done.1 = bf16[8,512,128]{2,1,0:T(8,128)(2,1)S(1)} async-done(((bf16[8,512,128]{2,1,0:T(8,128)(2,1)}), bf16[8,512,128]{2,1,0:T(8,128)(2,1)S(1)}, u32[]{:S(2)}, u32[]{:S(2)}) %all-to-all-start.1) | async-done | bytes 1048608 | tf_op jit(solution)/shard_map/all_to_all | solution.py:9
  30.2 0.1 copy_bitcast_fusion
  30.3 5.4 %gather_fusion.2 = bf16[1024,1024]{1,0:T(8,128)(2,1)} fusion(bf16[512,1024]{1,0:T(8,128)(2,1)S(1)} %copy_bitcast_fusion, s32[1024]{0:T(1024)S(1)} %fusion.21), kind=kCustom, calls=%fused_computation.1.clone | custom fusion | bytes 4198400 | tf_op jit(solution)/shard_map/jit(_take)/gather | solution.py:43
  35.7 7.6 %all-gather.2.cloned.1.call-done = bf16[512,1024]{1,0:T(8,128)(2,1)} async-done(((bf16[512,128]{1,0:T(8,128)(2,1)}), bf16[512,1024]{1,0:T(8,128)(2,1)}) %all-gather.2.cloned.1.call-update) | async-done | bytes 1048592 | tf_op jit(solution)/shard_map/all_gather | solution.py:57
  43.3 7.4 %gather_fusion.1 = bf16[1024,1024]{1,0:T(8,128)(2,1)} fusion(bf16[512,1024]{1,0:T(8,128)(2,1)} %all-gather.2.cloned.1.call-done, s32[1024]{0:T(1024)S(1)} %fusion.21), kind=kCustom, calls=%fused_computation.clone | custom fusion | bytes 4198400 | tf_op jit(solution)/shard_map/jit(_take)/gather | solution.py:43
  50.7 2.0 broadcast_select_fusion.1
  52.7 1.7 broadcast_select_fusion.3
  54.4 66.2 %all_to_all.20 = bf16[64,16,1024]{2,1,0:T(8,128)(2,1)S(1)} all-to-all(bf16[64,16,1024]{2,1,0:T(8,128)(2,1)S(1)} %get-tuple-element.5), channel_id=1, replica_groups=mesh['ep'=64,'tp'=8] {'ep'}, dimensions={0} | all-to-all | bytes 4194304 | tf_op jit(solution)/shard_map/all_to_all | solution.py:62
  120.7 8.6 %all-to-all-start = ((bf16[64,16,1024]{2,1,0:T(8,128)(2,1)}), bf16[64,16,1024]{2,1,0:T(8,128)(2,1)}, u32[]{:S(2)}, u32[]{:S(2)}) async-start(bf16[64,16,1024]{2,1,0:T(8,128)(2,1)} %get-tuple-element.4), calls=%async_computation | async-start | bytes 4194304 | tf_op jit(solution)/shard_map/all_to_all | solution.py:63
  129.3 2.6 fusion.11
  131.9 49.5 %all-to-all-done = bf16[64,16,1024]{2,1,0:T(8,128)(2,1)} async-done(((bf16[64,16,1024]{2,1,0:T(8,128)(2,1)}), bf16[64,16,1024]{2,1,0:T(8,128)(2,1)}, u32[]{:S(2)}, u32[]{:S(2)}) %all-to-all-start) | async-done | bytes 2097184 | tf_op jit(solution)/shard_map/all_to_all | solution.py:63
  181.5 4.9 %fusion.6 = bf16[1024,512]{1,0:T(8,128)(2,1)S(1)} fusion(f32[1024,512]{1,0:T(8,128)} %fusion.11, bf16[1024,1024]{1,0:T(8,128)(2,1)} %bitcast.4, bf16[1,512,1024]{2,1,0:T(8,128)(2,1)} %param.10), kind=kOutput, calls=%fused_computation.11 | convolution fusion | flops 1084227584 | bytes 6291456 | tf_op jit(solution)/shard_map/dot_general | solution.py:72
  186.4 1.0 copy-done.3
  187.4 3.2 %fusion.9 = f32[1024,1024]{1,0:T(8,128)} fusion(bf16[1024,512]{1,0:T(8,128)(2,1)S(1)} %fusion.6, bf16[1,1024,512]{2,1,0:T(8,128)(2,1)S(1)} %copy-done), kind=kOutput, calls=%fused_computation.22 | convolution fusion | flops 1073741824 | bytes 6291456 | tf_op jit(solution)/shard_map/dot_general | solution.py:82
  190.6 0.1 convert_reduce_fusion
  190.7 0.1 select_reduce_fusion
  190.9 38.8 %reduce-scatter.2.cloned.1.call-done = f32[1024,128]{1,0:T(8,128)} async-done(((f32[1024,1024]{1,0:T(8,128)}), f32[1024,128]{1,0:T(8,128)}) %reduce-scatter.2.cloned.1.call-update) | async-done | bytes 524304 | tf_op jit(solution)/shard_map/reduce_scatter | solution.py:85
  229.7 1.8 convert_element_type.20
  231.4 13.4 %all-to-all-start.3 = ((bf16[64,16,128]{2,1,0:T(8,128)(2,1)}), bf16[64,16,128]{2,1,0:T(8,128)(2,1)S(1)}, u32[]{:S(2)}, u32[]{:S(2)}) async-start(bf16[64,16,128]{2,1,0:T(8,128)(2,1)} %bitcast.49), calls=%async_computation.4 | async-start | bytes 524288 | tf_op jit(solution)/shard_map/all_to_all | solution.py:87
  244.8 3.6 %fusion.7 = bf16[1,1024,512]{2,1,0:T(8,128)(2,1)} fusion(bf16[1024,1024]{1,0:T(8,128)(2,1)S(1)} %bitcast.48, bf16[1024,512]{1,0:T(8,128)(2,1)} %copy-done.3), kind=kOutput, calls=%fused_computation.19 | convolution fusion | flops 1074266112 | bytes 4194304 | tf_op jit(solution)/shard_map/dot_general | solution.py:79
  248.4 4.0 %fusion.8 = bf16[1,512,1024]{2,1,0:T(8,128)(2,1)} fusion(bf16[1024,1024]{1,0:T(8,128)(2,1)} %bitcast.4, f32[1024,512]{1,0:T(8,128)S(1)} %copy-done.4), kind=kOutput, calls=%fused_computation.20 | convolution fusion | flops 1078984704 | bytes 5242880 | tf_op jit(solution)/shard_map/dot_general | solution.py:76
  252.4 5.4 %all-to-all-done.3 = bf16[64,16,128]{2,1,0:T(8,128)(2,1)S(1)} async-done(((bf16[64,16,128]{2,1,0:T(8,128)(2,1)}), bf16[64,16,128]{2,1,0:T(8,128)(2,1)S(1)}, u32[]{:S(2)}, u32[]{:S(2)}) %all-to-all-start.3) | async-done | bytes 262176 | tf_op jit(solution)/shard_map/all_to_all | solution.py:87
  257.8 1.3 gather_fusion
  259.1 0.8 broadcast_select_fusion.4
  (21 shorter events, 0.3 us)
Async XLA Ops:
  7.2 122.1 %copy-start = (bf16[1,1024,512]{2,1,0:T(8,128)(2,1)S(1)}, bf16[1,1024,512]{2,1,0:T(8,128)(2,1)}, u32[]{:S(2)}) copy-start(bf16[1,1024,512]{2,1,0:T(8,128)(2,1)} %param.9) | copy-start | bytes 3145732
  7.2 7.1 %copy-start.2 = (s32[1,64]{1,0:T(1,128)S(1)}, s32[1,64]{1,0:T(1,128)}, u32[]{:S(2)}) copy-start(s32[1,64]{1,0:T(1,128)} %param.11) | copy-start | bytes 772
  7.2 36.1 %all-gather.2.cloned.1.call-start = ((), (), s32[]{:S(2)}) async-start(), calls=%async_computation.5 | async-start | bytes 1179648 | tf_op jit(solution)/shard_map/all_gather | solution.py:57
  9.9 20.2 %all-to-all-start.1 = ((bf16[8,512,128]{2,1,0:T(8,128)(2,1)}), bf16[8,512,128]{2,1,0:T(8,128)(2,1)S(1)}, u32[]{:S(2)}, u32[]{:S(2)}) async-start(bf16[8,512,128]{2,1,0:T(8,128)(2,1)} %stack.2), calls=%async_computation.1 | async-start | bytes 2097152 | tf_op jit(solution)/shard_map/all_to_all | solution.py:9
  35.7 15.0 %copy-start.1 = (bf16[1024,1024]{1,0:T(8,128)(2,1)S(1)}, bf16[1024,1024]{1,0:T(8,128)(2,1)}, u32[]{:S(2)}) copy-start(bf16[1024,1024]{1,0:T(8,128)(2,1)} %gather_fusion.2) | copy-start | bytes 6291460
  120.7 60.8 %all-to-all-start = ((bf16[64,16,1024]{2,1,0:T(8,128)(2,1)}), bf16[64,16,1024]{2,1,0:T(8,128)(2,1)}, u32[]{:S(2)}, u32[]{:S(2)}) async-start(bf16[64,16,1024]{2,1,0:T(8,128)(2,1)} %get-tuple-element.4), calls=%async_computation | async-start | bytes 4194304 | tf_op jit(solution)/shard_map/all_to_all | solution.py:63
  129.3 100.4 %reduce-scatter.2.cloned.1.call-start = ((), (), s32[]{:S(2)}) async-start(), calls=%async_computation.6 | async-start | bytes 4718592 | tf_op jit(solution)/shard_map/reduce_scatter | solution.py:85
  186.4 1.0 copy-start.3
  231.4 26.4 %all-to-all-start.3 = ((bf16[64,16,128]{2,1,0:T(8,128)(2,1)}), bf16[64,16,128]{2,1,0:T(8,128)(2,1)S(1)}, u32[]{:S(2)}, u32[]{:S(2)}) async-start(bf16[64,16,128]{2,1,0:T(8,128)(2,1)} %bitcast.49), calls=%async_computation.4 | async-start | bytes 524288 | tf_op jit(solution)/shard_map/all_to_all | solution.py:87
  244.8 3.6 %copy-start.4 = (f32[1024,512]{1,0:T(8,128)S(1)}, f32[1024,512]{1,0:T(8,128)}, u32[]{:S(2)}) copy-start(f32[1024,512]{1,0:T(8,128)} %fusion.11) | copy-start | bytes 6291460
Sparse Core Ops, SparseCore 0:
  10.1 33.1 all-gather.1
  190.7 38.8 reduce-scatter.1
